TPU v7x, 32 devices: a whole 2x2x4 slice. The times are simulated.
32 devices in a mesh: dp: 8 (over z, y), tensor: 4 (over x, core).
Axes of the slice: x: 2, y: 2, z: 4, core: 2. Of those that a mesh axis runs over, the one named last changes fastest.
Arguments:
- layer_in: bfloat16 [4096, 1024], P(('dp', 'tensor')), may hold values from -6 to 6
- doc_pos: int32 [4096], P('dp'), may hold values from 0 to 1999, as said below
- gain_attend: float32 [1024], replicated, may hold values from 0.5 to 1.5
- shift_attend: float32 [1024], replicated, may hold values from -3 to 3
- gain_dense: float32 [1024], replicated, may hold values from 0.5 to 1.5
- shift_dense: float32 [1024], replicated, may hold values from -3 to 3
- w_qkv: bfloat16 [1024, 3072], P('dp', 'tensor')
- b_qkv: float32 [3072], P('tensor'), may hold values from -3 to 3
- w_out: bfloat16 [1024, 1024], P('tensor', 'dp'), may hold values from -0.75 to 0.75
- b_out: float32 [1024], replicated, may hold values from -3 to 3
- w_up: bfloat16 [1024, 4096], P('dp', 'tensor'), may hold values from -0.1875 to 0.1875
- b_up: float32 [4096], P('tensor'), may hold values from -3 to 3
- w_down: bfloat16 [4096, 1024], P('tensor', 'dp'), may hold values from -0.09375 to 0.09375
- b_down: float32 [1024], replicated, may hold values from -3 to 3
- grad_out: bfloat16 [4096, 1024], P(('dp', 'tensor')), may hold values from -6 to 6
Outputs:
- layer_out: bfloat16 [4096, 1024], P(('dp', 'tensor'))
- grad_in: float32 [4096, 1024], P(('dp', 'tensor'))
- dgain_attend: float32 [1024], replicated
- dshift_attend: float32 [1024], replicated
- dgain_dense: float32 [1024], replicated
- dshift_dense: float32 [1024], replicated
- dw_qkv: float32 [1024, 3072], P('dp', 'tensor')
- db_qkv: float32 [3072], P('tensor')
- dw_out: float32 [1024, 1024], P('tensor', 'dp')
- db_out: float32 [1024], replicated
- dw_up: float32 [1024, 4096], P('dp', 'tensor')
- db_up: float32 [4096], P('tensor')
- dw_down: float32 [4096, 1024], P('tensor', 'dp')
- db_down: float32 [1024], replicated
Inputs may be any that keep to these rules, and one draw needn't show every extreme that they name: `doc_pos`: positions rise by one from token to token and restart at 0 where a document begins; the first token is at position 0; every whole document has 200 to 2000 tokens and one has exactly 2000; the last may be cut short, and a document may run across the border of two packed sequences.
All inputs are finite; a program needn't handle non-finite values.
Results may differ from a plain program's by a relative error of at most 0.02.
The roundings to bfloat16 on the way count: a program that leaves them out, or rounds other values in their place, can miss the bound.
Values may be sent and summed in bfloat16 or wider, within the bound.
No kernel may reach another device: no remote copies, remote signals or barrier semaphores. Data moves between devices by JAX's collectives and lax.ppermute only.
A program may use at most 128 MiB of HBM per device.

v0:
```python
import jax
import jax.numpy as jnp
from jax import lax
from jax.sharding import PartitionSpec as P

HEADS = 16
HD = 64
ROT = 16
SEQ = 4096
REACH = 4
EPS = 1e-05
MASKED = -1e30


def shifted_2(shard, axis, by):
    count = lax.axis_size(axis)
    pairs = [(i, i + by) for i in range(count) if 0 <= i + by < count]
    return lax.ppermute(shard, axis, pairs)


def normalize(x_float):
    average = jnp.mean(x_float, axis=-1, keepdims=True)
    centred = x_float - average
    inv_std = lax.rsqrt(jnp.mean(centred * centred, axis=-1, keepdims=True) + EPS)
    return (centred * inv_std, inv_std)


def norm_back(dnormed, normed, inv_std):
    return inv_std * (
        dnormed
        - jnp.mean(dnormed, axis=-1, keepdims=True)
        - normed * jnp.mean(dnormed * normed, axis=-1, keepdims=True)
    )


def rotary_tables(positions):
    half_rot = ROT // 2
    inv_freq = jnp.power(10000.0, -2.0 * jnp.arange(half_rot, dtype=jnp.float32) / ROT)
    angles = positions.astype(jnp.float32)[:, None] * inv_freq[None, :]
    cos_tab = jnp.cos(angles)
    sin_tab = jnp.sin(angles)
    return (
        jnp.concatenate([cos_tab, cos_tab], axis=-1),
        jnp.concatenate([sin_tab, sin_tab], axis=-1),
    )


def rotate(vectors, cos_tab, sin_tab):
    half_rot = ROT // 2
    leading = vectors[..., :ROT]
    turned = jnp.concatenate([-leading[..., half_rot:], leading[..., :half_rot]], axis=-1)
    return jnp.concatenate([leading * cos_tab + turned * sin_tab, vectors[..., ROT:]], axis=-1)


def rotate_back(upstream, cos_tab, sin_tab):
    half_rot = ROT // 2
    leading = upstream[..., :ROT]
    shifted = leading * sin_tab
    turned = jnp.concatenate([shifted[..., half_rot:], -shifted[..., :half_rot]], axis=-1)
    return jnp.concatenate([leading * cos_tab + turned, upstream[..., ROT:]], axis=-1)


def gelu_slope(preact):
    return (
        0.5 * (1.0 + lax.erf(preact * 0.7071067811865476))
        + preact * jnp.exp(-0.5 * preact * preact) * 0.3989422804014327
    )


def rows_product(left_rows, right_rows):
    return lax.dot_general(
        left_rows, right_rows, (((0,), (0,)), ((), ())), preferred_element_type=jnp.float32
    )


def shards(
    layer_in,
    doc_pos,
    gain_attend,
    shift_attend,
    gain_dense,
    shift_dense,
    w_qkv,
    b_qkv,
    w_out,
    b_out,
    w_up,
    b_up,
    w_down,
    b_down,
    grad_out,
):
    local_heads = HEADS // lax.axis_size("tensor")
    head_width = local_heads * HD
    score_scale = HD ** (-0.5)
    x_float = layer_in.astype(jnp.float32)
    normed, inv_std = normalize(x_float)
    first_in, second_in = (
        lax.all_gather(
            (normed * gain_attend + shift_attend).astype(jnp.bfloat16), "tensor", axis=0, tiled=True
        ),
        lax.all_gather(
            (normed * gain_dense + shift_dense).astype(jnp.bfloat16), "tensor", axis=0, tiled=True
        ),
    )
    row_count = first_in.shape[0]
    weights = (
        lax.all_gather(w_qkv, "dp", axis=0, tiled=True),
        lax.all_gather(w_out, "dp", axis=1, tiled=True),
        lax.all_gather(w_up, "dp", axis=0, tiled=True),
        lax.all_gather(w_down, "dp", axis=1, tiled=True),
    )
    full_qkv, full_out, full_up, full_down = weights
    joined_qkv = (jnp.dot(first_in, full_qkv, preferred_element_type=jnp.float32) + b_qkv).reshape(
        row_count, local_heads, 3, HD
    )
    cos_tab, sin_tab = rotary_tables(doc_pos)
    cos_tab = cos_tab[:, None, :]
    sin_tab = sin_tab[:, None, :]
    queries = rotate(joined_qkv[:, :, 0], cos_tab, sin_tab).astype(jnp.bfloat16)
    keys_rot = rotate(joined_qkv[:, :, 1], cos_tab, sin_tab).astype(jnp.bfloat16)
    values = joined_qkv[:, :, 2].astype(jnp.bfloat16)
    own_pair = jnp.stack(
        [keys_rot.reshape(row_count, head_width), values.reshape(row_count, head_width)], axis=0
    )
    key_pairs = [own_pair]
    for distance in range(1, REACH + 1):
        key_pairs.append(shifted_2(own_pair, "dp", distance))
    query_at = lax.axis_index("dp") * row_count + jnp.arange(row_count, dtype=jnp.int32)
    block_masks = []
    for distance in range(REACH + 1):
        key_at = query_at - distance * row_count
        offsets = query_at[:, None] - key_at[None, :]
        block_masks.append(
            (offsets >= 0)
            & (offsets <= doc_pos[:, None])
            & (query_at[:, None] // SEQ == key_at[None, :] // SEQ)
        )

    def block_scores(key_pair, allowed):
        keys_blk = key_pair[0].reshape(row_count, local_heads, HD)
        raw_scores = (
            jnp.einsum("qhd,khd->hqk", queries, keys_blk, preferred_element_type=jnp.float32)
            * score_scale
        )
        return jnp.where(allowed[None], raw_scores, MASKED)

    all_scores = [
        block_scores(key_pair, allowed) for key_pair, allowed in zip(key_pairs, block_masks)
    ]
    row_peak = all_scores[0].max(axis=-1)
    for scores in all_scores[1:]:
        row_peak = jnp.maximum(row_peak, scores.max(axis=-1))
    row_total = jnp.zeros_like(row_peak)
    for scores in all_scores:
        row_total = row_total + jnp.sum(jnp.exp(scores - row_peak[..., None]), axis=-1)
    logsum = row_peak + jnp.log(row_total)
    context = jnp.zeros((row_count, local_heads, HD), jnp.float32)
    for scores, key_pair in zip(all_scores, key_pairs):
        softmax = jnp.exp(scores - logsum[..., None]).astype(jnp.bfloat16)
        context = context + jnp.einsum(
            "hqk,khd->qhd",
            softmax,
            key_pair[1].reshape(row_count, local_heads, HD),
            preferred_element_type=jnp.float32,
        )
    context_b = context.reshape(row_count, head_width).astype(jnp.bfloat16)
    preact = jnp.dot(second_in, full_up, preferred_element_type=jnp.float32) + b_up
    hidden = jax.nn.gelu(preact, approximate=False).astype(jnp.bfloat16)
    branch = lax.psum_scatter(
        jnp.dot(context_b, full_out, preferred_element_type=jnp.float32)
        + jnp.dot(hidden, full_down, preferred_element_type=jnp.float32),
        "tensor",
        scatter_dimension=0,
        tiled=True,
    )
    layer_out = (x_float + b_out + b_down + branch).astype(jnp.bfloat16)
    grad_rows = lax.all_gather(grad_out, "tensor", axis=0, tiled=True)
    back_weights = (
        lax.all_gather(w_qkv, "dp", axis=0, tiled=True),
        lax.all_gather(w_out, "dp", axis=1, tiled=True),
        lax.all_gather(w_up, "dp", axis=0, tiled=True),
        lax.all_gather(w_down, "dp", axis=1, tiled=True),
    )
    back_qkv, back_out, back_up, back_down = back_weights
    dcontext = jnp.dot(grad_rows, back_out.T, preferred_element_type=jnp.float32).astype(
        jnp.bfloat16
    )
    dpreact = jnp.dot(grad_rows, back_down.T, preferred_element_type=jnp.float32) * gelu_slope(
        preact
    )
    dpreact_b = dpreact.astype(jnp.bfloat16)
    dw_out, dw_up, dw_down = (
        lax.psum_scatter(rows_product(context_b, grad_rows), "dp", scatter_dimension=1, tiled=True),
        lax.psum_scatter(rows_product(second_in, dpreact_b), "dp", scatter_dimension=0, tiled=True),
        lax.psum_scatter(rows_product(hidden, grad_rows), "dp", scatter_dimension=1, tiled=True),
    )
    dctx_heads = dcontext.reshape(row_count, local_heads, HD)
    deltas = jnp.sum(
        dctx_heads.astype(jnp.float32)
        * context_b.reshape(row_count, local_heads, HD).astype(jnp.float32),
        axis=-1,
    ).T
    dqueries = jnp.zeros((row_count, local_heads, HD), jnp.float32)
    pair_grads = []
    for key_pair, allowed in zip(key_pairs, block_masks):
        keys_blk = key_pair[0].reshape(row_count, local_heads, HD)
        values_blk = key_pair[1].reshape(row_count, local_heads, HD)
        scores = block_scores(key_pair, allowed)
        softmax_f = jnp.exp(scores - logsum[..., None])
        softmax_b = softmax_f.astype(jnp.bfloat16)
        dvalues = jnp.einsum(
            "hqk,qhd->khd", softmax_b, dctx_heads, preferred_element_type=jnp.float32
        )
        dsoftmax = jnp.einsum(
            "qhd,khd->hqk", dctx_heads, values_blk, preferred_element_type=jnp.float32
        )
        dscores = (softmax_f * (dsoftmax - deltas[..., None]) * score_scale).astype(jnp.bfloat16)
        dqueries = dqueries + jnp.einsum(
            "hqk,khd->qhd", dscores, keys_blk, preferred_element_type=jnp.float32
        )
        dkeys = jnp.einsum("hqk,qhd->khd", dscores, queries, preferred_element_type=jnp.float32)
        pair_grads.append(
            jnp.stack(
                [dkeys.reshape(row_count, head_width), dvalues.reshape(row_count, head_width)],
                axis=0,
            )
        )
    pair_total = pair_grads[0]
    for distance in range(1, REACH + 1):
        pair_total = pair_total + shifted_2(pair_grads[distance], "dp", -distance)
    dq_pre = rotate_back(dqueries, cos_tab, sin_tab)
    dk_pre = rotate_back(pair_total[0].reshape(row_count, local_heads, HD), cos_tab, sin_tab)
    dfused = jnp.stack(
        [dq_pre, dk_pre, pair_total[1].reshape(row_count, local_heads, HD)], axis=2
    ).reshape(row_count, 3 * head_width)
    bqkv_part = jnp.sum(dfused, axis=0)
    dfused_b = dfused.astype(jnp.bfloat16)
    dnorms = lax.psum_scatter(
        jnp.stack(
            [
                jnp.dot(dfused_b, back_qkv.T, preferred_element_type=jnp.float32),
                jnp.dot(dpreact_b, back_up.T, preferred_element_type=jnp.float32),
            ],
            axis=1,
        ),
        "tensor",
        scatter_dimension=0,
        tiled=True,
    )
    dfirst = dnorms[:, 0]
    dsecond = dnorms[:, 1]
    grad_float = grad_out.astype(jnp.float32)
    grad_in = grad_float + norm_back(dfirst * gain_attend + dsecond * gain_dense, normed, inv_std)
    dw_qkv = lax.psum_scatter(
        rows_product(first_in, dfused_b), "dp", scatter_dimension=0, tiled=True
    )
    db_qkv, db_up = lax.psum((bqkv_part, jnp.sum(dpreact, axis=0)), "dp")
    norm_sums = lax.psum(
        (
            jnp.sum(dfirst * normed, axis=0),
            jnp.sum(dfirst, axis=0),
            jnp.sum(dsecond * normed, axis=0),
            jnp.sum(dsecond, axis=0),
            jnp.sum(grad_float, axis=0),
        ),
        ("dp", "tensor"),
    )
    return (
        layer_out,
        grad_in,
        norm_sums[0],
        norm_sums[1],
        norm_sums[2],
        norm_sums[3],
        dw_qkv,
        db_qkv,
        dw_out,
        norm_sums[4],
        dw_up,
        db_up,
        dw_down,
        norm_sums[4],
    )


def solution(mesh):
    return jax.shard_map(
        shards,
        mesh=mesh,
        in_specs=(
            P(("dp", "tensor"), None),
            P("dp"),
            P(),
            P(),
            P(),
            P(),
            P("dp", "tensor"),
            P("tensor"),
            P("tensor", "dp"),
            P(),
            P("dp", "tensor"),
            P("tensor"),
            P("tensor", "dp"),
            P(),
            P(("dp", "tensor"), None),
        ),
        out_specs=(
            P(("dp", "tensor"), None),
            P(("dp", "tensor"), None),
            P(),
            P(),
            P(),
            P(),
            P("dp", "tensor"),
            P("tensor"),
            P("tensor", "dp"),
            P(),
            P("dp", "tensor"),
            P("tensor"),
            P("tensor", "dp"),
            P(),
        ),
        check_vma=False,
    )
```

profile of v0, /device:TPU:0, one launch (start us, length us, event | category | flops | bytes accessed | tf_op | source)
XLA Modules:
  0.0 799.1 jit_solution(18386472746760423022)
XLA Ops:
  10.2 2.0 fusion.55
  15.0 29.6 %all_gather.27 = bf16[256,1024]{1,0:T(8,128)(2,1)S(1)} all-gather(bf16[256,128]{1,0:T(8,128)(2,1)S(1)} %copy-done.17), channel_id=1, replica_groups=mesh['dp'=8,'tensor'=4] {'dp'}, dimensions={1}, use_global_device_ids=true | all-gather | bytes 589824 | tf_op jit(solution)/shard_map/all_gather | solution.py:109
  44.7 2.7 fusion.39
  47.4 2.4 convolution_convert_fusion
  49.8 44.5 %all-gather.9.cloned.1.call-done = bf16[1024,768]{1,0:T(8,128)(2,1)} async-done(((bf16[128,768]{1,0:T(8,128)(2,1)}), bf16[1024,768]{1,0:T(8,128)(2,1)}) %all-gather.9.cloned.1.call-update) | async-done | bytes 1572880 | tf_op jit(solution)/shard_map/all_gather | solution.py:108
  94.3 2.7 convolution_add_fusion.1
  97.9 2.5 collective-permute-start
  100.4 3.4 collective-permute-start.1
  103.8 3.6 collective-permute-start.2
  107.4 1.3 collective-permute-start.3
  111.5 4.5 collective-permute-done.1
  117.0 15.4 %collective-permute-done.2 = bf16[2,512,256]{1,2,0:T(8,128)(2,1)S(1)} collective-permute-done((bf16[2,512,256]{1,2,0:T(8,128)(2,1)S(1)}, bf16[2,512,256]{1,2,0:T(8,128)(2,1)S(1)}, u32[]{:S(2)}, u32[]{:S(2)}) %collective-permute-start.2) | collective-permute-done | bytes 524320 | tf_op jit(solution)/shard_map/ppermute | solution.py:18
  133.4 10.9 %collective-permute-done.3 = bf16[2,512,256]{1,2,0:T(8,128)(2,1)S(1)} collective-permute-done((bf16[2,512,256]{1,2,0:T(8,128)(2,1)S(1)}, bf16[2,512,256]{1,2,0:T(8,128)(2,1)S(1)}, u32[]{:S(2)}, u32[]{:S(2)}) %collective-permute-start.3) | collective-permute-done | bytes 524320 | tf_op jit(solution)/shard_map/ppermute | solution.py:18
  145.3 5.1 exponential_reduce_fusion.3
  155.5 2.0 multiply_reduce_fusion
  157.5 1.6 multiply_convert_fusion.4
  159.2 1.6 multiply_convert_fusion.3
  160.8 1.6 multiply_convert_fusion.1
  162.4 1.6 multiply_convert_fusion
  164.1 1.8 multiply_convert_fusion.2
  172.8 1.3 collective-permute-start.4
  175.9 1.3 collective-permute-start.5
  179.0 1.3 collective-permute-start.6
  182.1 1.3 collective-permute-start.7
  188.4 8.8 %fusion.12 = (bf16[512,1024]{1,0:T(8,128)(2,1)}, f32[512,1024]{1,0:T(8,128)}) fusion(f32[1024]{0:T(1024)S(1)} %copy-done.27, bf16[512,1024]{1,0:T(8,128)(2,1)} %all-gather.11.cloned.1.call-done, bf16[1024,1024]{1,0:T(8,128)(2,1)} %all-gather.13.cloned.1.call-done), kind=kOutput, calls=%fused_computation.35 | convolution fusion | flops 1108344832 | bytes 6295552 | tf_op jit(solution)/shard_map/dot_general | solution.py:168
  197.2 66.6 %all-gather.15.cloned.1.call-done = bf16[1024,1024]{1,0:T(8,128)(2,1)} async-done(((bf16[1024,128]{1,0:T(8,128)(2,1)}), bf16[1024,1024]{1,0:T(8,128)(2,1)}) %all-gather.15.cloned.1.call-update) | async-done | bytes 2097168 | tf_op jit(solution)/shard_map/all_gather | solution.py:111
  263.8 4.2 fusion.129
  268.0 1.3 convolution_bitcast_fusion
  269.3 21.3 %collective-permute-done.6 = f32[2,512,256]{1,2,0:T(8,128)} collective-permute-done((f32[2,512,256]{1,2,0:T(8,128)}, f32[2,512,256]{1,2,0:T(8,128)}, u32[]{:S(2)}, u32[]{:S(2)}) %collective-permute-start.6) | collective-permute-done | bytes 1048608 | tf_op jit(solution)/shard_map/ppermute | solution.py:18
  290.7 86.4 %collective-permute-done.7 = f32[2,512,256]{1,2,0:T(8,128)} collective-permute-done((f32[2,512,256]{1,2,0:T(8,128)}, f32[2,512,256]{1,2,0:T(8,128)}, u32[]{:S(2)}, u32[]{:S(2)}) %collective-permute-start.7) | collective-permute-done | bytes 1048608 | tf_op jit(solution)/shard_map/ppermute | solution.py:18
  377.1 2.8 fusion.35
  382.7 2.3 pad_maximum_fusion
  385.0 3.2 fusion.133
  388.3 1.8 convolution_add_fusion
  390.1 2.4 fusion.137
  392.6 4.0 fusion.136
  396.7 4.9 fusion.69
  401.9 4.5 fusion.138
  406.7 17.9 %all-reduce.1 = (f32[768]{0:T(1024)}, f32[1024]{0:T(1024)}) all-reduce(f32[768]{0:T(1024)S(1)} %reduce_sum.170, f32[1024]{0:T(1024)S(1)} %get-tuple-element.85), channel_id=1, replica_groups=mesh['dp'=8,'tensor'=4] {'dp'}, use_global_device_ids=true, to_apply=%region_27.28 | all-reduce | flops 1792 | bytes 14336 | tf_op jit(solution)/shard_map/psum | solution.py:258
  424.7 2.2 reduce-scatter.9.cloned.1.call-done
  428.2 1.5 fusion.120
  429.7 30.9 %reduce-scatter.7.cloned.1.call-done = f32[128,1024]{1,0:T(8,128)} async-done(((f32[512,1024]{1,0:T(8,128)}), f32[128,1024]{1,0:T(8,128)}) %reduce-scatter.7.cloned.1.call-update) | async-done | bytes 524304 | tf_op jit(solution)/shard_map/reduce_scatter | solution.py:170
  460.6 2.1 convert_reduce_fusion.1
  462.8 39.8 %all-reduce = (f32[1024]{0:T(1024)}, f32[1024]{0:T(1024)}, f32[1024]{0:T(1024)}, f32[1024]{0:T(1024)}, f32[1024]{0:T(1024)S(1)}) all-reduce(f32[1024]{0:T(1024)S(1)} %get-tuple-element.20, f32[1024]{0:T(1024)S(1)} %get-tuple-element.17, f32[1024]{0:T(1024)S(1)} %get-tuple-element.21, ...), channel_id=1, replica_groups=mesh['dp'=8,'tensor'=4] {'dp','tensor'}, use_global_device_ids=true, to_apply=%region_18.19 | all-reduce | flops 5120 | bytes 40960 | tf_op jit(solution)/shard_map/psum | solution.py:259
  502.5 27.6 %reduce-scatter.13.cloned.1.call-done = f32[256,128]{1,0:T(8,128)} async-done(((f32[256,1024]{1,0:T(8,128)}), f32[256,128]{1,0:T(8,128)}) %reduce-scatter.13.cloned.1.call-update) | async-done | bytes 131088 | tf_op jit(solution)/shard_map/reduce_scatter | solution.py:194
  530.1 77.3 %reduce-scatter.11.cloned.1.call-done = f32[128,768]{1,0:T(8,128)} async-done(((f32[1024,768]{1,0:T(8,128)}), f32[128,768]{1,0:T(8,128)}) %reduce-scatter.11.cloned.1.call-update) | async-done | bytes 393232 | tf_op jit(solution)/shard_map/reduce_scatter | solution.py:255
  607.4 91.6 %reduce-scatter.15.cloned.1.call-done = f32[128,1024]{1,0:T(8,128)} async-done(((f32[1024,1024]{1,0:T(8,128)}), f32[128,1024]{1,0:T(8,128)}) %reduce-scatter.15.cloned.1.call-update) | async-done | bytes 524304 | tf_op jit(solution)/shard_map/reduce_scatter | solution.py:195
  699.0 92.5 %reduce-scatter.17.cloned.1.call-done = f32[1024,128]{1,0:T(8,128)} async-done(((f32[1024,1024]{1,0:T(8,128)}), f32[1024,128]{1,0:T(8,128)}) %reduce-scatter.17.cloned.1.call-update) | async-done | bytes 524304 | tf_op jit(solution)/shard_map/reduce_scatter | solution.py:196
  (165 shorter events, 39.7 us)
Async XLA Ops:
  7.2 7.8 copy-start.20
  7.2 7.8 copy-start.17
  7.2 40.2 %all-gather.17.cloned.1.call-start = ((), (), s32[]{:S(2)}) async-start(), calls=%async_computation.12 | async-start | bytes 1310720 | tf_op jit(solution)/shard_map/all_gather | solution.py:178
  7.9 41.9 %all-gather.7.cloned.1.call-start = ((), (), s32[]{:S(2)}) async-start(), calls=%async_computation.6 | async-start | bytes 1310720 | tf_op jit(solution)/shard_map/all_gather | solution.py:99
  12.3 82.0 %all-gather.9.cloned.1.call-start = ((), (), s32[]{:S(2)}) async-start(), calls=%async_computation.7 | async-start | bytes 1769472 | tf_op jit(solution)/shard_map/all_gather | solution.py:108
  13.0 175.3 %all-gather.11.cloned.1.call-start = ((), (), s32[]{:S(2)}) async-start(), calls=%async_computation.8 | async-start | bytes 1310720 | tf_op jit(solution)/shard_map/all_gather | solution.py:102
  13.6 174.8 %all-gather.13.cloned.1.call-start = ((), (), s32[]{:S(2)}) async-start(), calls=%async_computation.9 | async-start | bytes 2359296 | tf_op jit(solution)/shard_map/all_gather | solution.py:110
  14.2 80.1 %copy-start.26 = (f32[768]{0:T(1024)S(1)}, f32[768]{0:T(1024)}, u32[]{:S(2)}) copy-start(f32[768]{0:T(1024)} %param.22) | copy-start | bytes 9220
  14.2 249.6 %all-gather.15.cloned.1.call-start = ((), (), s32[]{:S(2)}) async-start(), calls=%async_computation.10 | async-start | bytes 2359296 | tf_op jit(solution)/shard_map/all_gather | solution.py:111
  14.8 412.1 %reduce-scatter.9.cloned.1.call-start = ((), (), s32[]{:S(2)}) async-start(), calls=%async_computation.13 | async-start | bytes 5242880 | tf_op jit(solution)/shard_map/reduce_scatter | solution.py:239
  44.5 49.8 %copy-start.2 = (bf16[256,1024]{1,0:T(8,128)(2,1)}, bf16[256,1024]{1,0:T(8,128)(2,1)S(1)}, u32[]{:S(2)}) copy-start(bf16[256,1024]{1,0:T(8,128)(2,1)S(1)} %all_gather.27) | copy-start | bytes 1572868
  97.9 12.6 %collective-permute-start = (bf16[2,512,256]{1,2,0:T(8,128)(2,1)S(1)}, bf16[2,512,256]{1,2,0:T(8,128)(2,1)S(1)}, u32[]{:S(2)}, u32[]{:S(2)}) collective-permute-start(bf16[2,512,256]{1,2,0:T(8,128)(2,1)S(1)} %pad_maximum_fusion.6), channel_id=1, source_target_pairs={{0,4},{4,8},{8,12},{12,16},{16,20},{20,24},{24,28},{1,5},{5,9},{9,... | collective-permute-start | bytes 1572872 | tf_op jit(solution)/shard_map/ppermute | solution.py:18
  100.4 15.6 %collective-permute-start.1 = (bf16[2,512,256]{1,2,0:T(8,128)(2,1)S(1)}, bf16[2,512,256]{1,2,0:T(8,128)(2,1)S(1)}, u32[]{:S(2)}, u32[]{:S(2)}) collective-permute-start(bf16[2,512,256]{1,2,0:T(8,128)(2,1)S(1)} %pad_maximum_fusion.6), channel_id=1, source_target_pairs={{0,8},{4,12},{8,16},{12,20},{16,24},{20,28},{1,9},{5,13},{9,17},{1... | collective-permute-start | bytes 1572872 | tf_op jit(solution)/shard_map/ppermute | solution.py:18
  103.8 28.7 %collective-permute-start.2 = (bf16[2,512,256]{1,2,0:T(8,128)(2,1)S(1)}, bf16[2,512,256]{1,2,0:T(8,128)(2,1)S(1)}, u32[]{:S(2)}, u32[]{:S(2)}) collective-permute-start(bf16[2,512,256]{1,2,0:T(8,128)(2,1)S(1)} %pad_maximum_fusion.6), channel_id=1, source_target_pairs={{0,12},{4,16},{8,20},{12,24},{16,28},{1,13},{5,17},{9,21},{13,25},... | collective-permute-start | bytes 1572872 | tf_op jit(solution)/shard_map/ppermute | solution.py:18
  107.4 36.9 %collective-permute-start.3 = (bf16[2,512,256]{1,2,0:T(8,128)(2,1)S(1)}, bf16[2,512,256]{1,2,0:T(8,128)(2,1)S(1)}, u32[]{:S(2)}, u32[]{:S(2)}) collective-permute-start(bf16[2,512,256]{1,2,0:T(8,128)(2,1)S(1)} %pad_maximum_fusion.6), channel_id=1, source_target_pairs={{0,16},{4,20},{8,24},{12,28},{1,17},{5,21},{9,25},{13,29},{2,18},{... | collective-permute-start | bytes 1572872 | tf_op jit(solution)/shard_map/ppermute | solution.py:18
  108.8 1.8 copy-start.7
  110.6 5.5 copy-start.6
  116.1 39.4 %copy-start.15 = (bf16[1,512,256]{1,2,0:T(8,128)(2,1)}, bf16[1,512,256]{1,2,0:T(8,128)(2,1)S(1)}, u32[]{:S(2)}) copy-start(bf16[1,512,256]{1,2,0:T(8,128)(2,1)S(1)} %get-tuple-element.39) | copy-start | bytes 786436
  116.1 16.4 %copy-start.5 = (pred[512,512]{0,1:T(8,128)(4,1)S(1)}, pred[512,512]{0,1:T(8,128)(4,1)}, u32[]{:S(2)}) copy-start(pred[512,512]{0,1:T(8,128)(4,1)} %get-tuple-element.66) | copy-start | bytes 786436
  132.5 1.0 copy-start.10
  132.5 11.9 %copy-start.4 = (pred[512,512]{0,1:T(8,128)(4,1)S(1)}, pred[512,512]{0,1:T(8,128)(4,1)}, u32[]{:S(2)}) copy-start(pred[512,512]{0,1:T(8,128)(4,1)} %get-tuple-element.67) | copy-start | bytes 786436
  154.2 1.3 copy-start.28
  162.4 1.6 copy-start.16
  172.8 96.5 %collective-permute-start.4 = (f32[2,512,256]{1,2,0:T(8,128)}, f32[2,512,256]{1,2,0:T(8,128)}, u32[]{:S(2)}, u32[]{:S(2)}) collective-permute-start(f32[2,512,256]{1,2,0:T(8,128)} %pad_maximum_fusion.2), channel_id=1, source_target_pairs={{4,0},{8,4},{12,8},{16,12},{20,16},{24,20},{28,24},{5,1},{9,5},{13... | collective-permute-start | bytes 3145736 | tf_op jit(solution)/shard_map/ppermute | solution.py:18
  175.9 93.5 %collective-permute-start.5 = (f32[2,512,256]{1,2,0:T(8,128)}, f32[2,512,256]{1,2,0:T(8,128)}, u32[]{:S(2)}, u32[]{:S(2)}) collective-permute-start(f32[2,512,256]{1,2,0:T(8,128)} %pad_maximum_fusion.3), channel_id=1, source_target_pairs={{8,0},{12,4},{16,8},{20,12},{24,16},{28,20},{9,1},{13,5},{17,9},{2... | collective-permute-start | bytes 3145736 | tf_op jit(solution)/shard_map/ppermute | solution.py:18
  179.0 111.7 %collective-permute-start.6 = (f32[2,512,256]{1,2,0:T(8,128)}, f32[2,512,256]{1,2,0:T(8,128)}, u32[]{:S(2)}, u32[]{:S(2)}) collective-permute-start(f32[2,512,256]{1,2,0:T(8,128)} %pad_maximum_fusion.4), channel_id=1, source_target_pairs={{12,0},{16,4},{20,8},{24,12},{28,16},{13,1},{17,5},{21,9},{25,13},... | collective-permute-start | bytes 3145736 | tf_op jit(solution)/shard_map/ppermute | solution.py:18
  181.0 2.9 copy-start.11
  182.1 195.0 %collective-permute-start.7 = (f32[2,512,256]{1,2,0:T(8,128)}, f32[2,512,256]{1,2,0:T(8,128)}, u32[]{:S(2)}, u32[]{:S(2)}) collective-permute-start(f32[2,512,256]{1,2,0:T(8,128)} %pad_maximum_fusion.5), channel_id=1, source_target_pairs={{16,0},{20,4},{24,8},{28,12},{17,1},{21,5},{25,9},{29,13},{18,2},{... | collective-permute-start | bytes 3145736 | tf_op jit(solution)/shard_map/ppermute | solution.py:18
  183.9 1.0 copy-start.13
  187.1 1.3 copy-start.27
  188.3 75.5 %copy-start.1 = (bf16[512,1024]{1,0:T(8,128)(2,1)S(1)}, bf16[512,1024]{1,0:T(8,128)(2,1)}, u32[]{:S(2)}) copy-start(bf16[512,1024]{1,0:T(8,128)(2,1)} %all-gather.17.cloned.1.call-done) | copy-start | bytes 3145732
  263.8 4.2 copy-start.24
  268.0 1.3 copy-start.14
  380.2 1.4 copy-start.25
  385.0 75.7 %reduce-scatter.7.cloned.1.call-start = ((), (), s32[]{:S(2)}) async-start(), calls=%async_computation.11 | async-start | bytes 2621440 | tf_op jit(solution)/shard_map/reduce_scatter | solution.py:170
  385.0 3.3 copy-start.3
  385.0 3.3 copy-start.8
  390.1 140.0 %reduce-scatter.13.cloned.1.call-start = ((), (), s32[]{:S(2)}) async-start(), calls=%async_computation.15 | async-start | bytes 1179648 | tf_op jit(solution)/shard_map/reduce_scatter | solution.py:194
  392.6 214.8 %reduce-scatter.11.cloned.1.call-start = ((), (), s32[]{:S(2)}) async-start(), calls=%async_computation.14 | async-start | bytes 3538944 | tf_op jit(solution)/shard_map/reduce_scatter | solution.py:255
  396.7 302.4 %reduce-scatter.15.cloned.1.call-start = ((), (), s32[]{:S(2)}) async-start(), calls=%async_computation.16 | async-start | bytes 4718592 | tf_op jit(solution)/shard_map/reduce_scatter | solution.py:195
  401.7 389.8 %reduce-scatter.17.cloned.1.call-start = ((), (), s32[]{:S(2)}) async-start(), calls=%async_computation.17 | async-start | bytes 4718592 | tf_op jit(solution)/shard_map/reduce_scatter | solution.py:196
  406.4 21.8 %copy-start = (bf16[128,1024]{1,0:T(8,128)(2,1)S(1)}, bf16[128,1024]{1,0:T(8,128)(2,1)}, u32[]{:S(2)}) copy-start(bf16[128,1024]{1,0:T(8,128)(2,1)} %param.15) | copy-start | bytes 786436
  406.4 21.8 %copy-start.18 = (f32[1024]{0:T(1024)S(1)}, f32[1024]{0:T(1024)}, u32[]{:S(2)}) copy-start(f32[1024]{0:T(1024)} %param.17) | copy-start | bytes 12292
  406.4 21.8 %copy-start.19 = (f32[1024]{0:T(1024)S(1)}, f32[1024]{0:T(1024)}, u32[]{:S(2)}) copy-start(f32[1024]{0:T(1024)} %param.19) | copy-start | bytes 12292
  406.4 54.2 %copy-start.9 = (bf16[128,1024]{1,0:T(8,128)(2,1)S(1)}, bf16[128,1024]{1,0:T(8,128)(2,1)}, u32[]{:S(2)}) copy-start(bf16[128,1024]{1,0:T(8,128)(2,1)} %param.29) | copy-start | bytes 786436
  406.4 54.2 %copy-start.21 = (f32[1024]{0:T(1024)S(1)}, f32[1024]{0:T(1024)}, u32[]{:S(2)}) copy-start(f32[1024]{0:T(1024)} %param.28) | copy-start | bytes 12292
  406.5 54.2 %copy-start.22 = (f32[1024]{0:T(1024)S(1)}, f32[1024]{0:T(1024)}, u32[]{:S(2)}) copy-start(f32[1024]{0:T(1024)} %param.24) | copy-start | bytes 12292
  502.5 289.6 %copy-start.23 = (f32[1024]{0:T(1024)}, f32[1024]{0:T(1024)S(1)}, u32[]{:S(2)}) copy-start(f32[1024]{0:T(1024)S(1)} %get-tuple-element.130) | copy-start | bytes 12292
  (1 other events, 0.9 us)
Sparse Core Ops, SparseCore 0:
  9.6 19.4 all-gather.16
  31.2 16.6 all-gather.6
  50.1 44.2 all-gather.8
  96.3 15.0 all-gather.10
  113.4 72.5 all-gather.12
  187.8 75.9 all-gather.14
  385.1 41.7 reduce-scatter.8
  429.4 31.1 reduce-scatter.6
  464.6 65.4 reduce-scatter.12
  534.1 73.2 reduce-scatter.10
  611.6 87.3 reduce-scatter.14
  703.1 88.3 reduce-scatter.16
where the time goes:
time: 807 us; the launch traced here: 799 us
  waiting for transfers between devices  576 us (71%)
  blocking collectives  87.3 us (11%)
  matrix products  73.6 us (9%)
  other arithmetic  27.3 us (3%)
  starting transfers between devices  16.6 us (2%)
  between operations  15.3 us (2%)
    ppermute x8, waiting for transfers between devices, shifted_2(): return lax.ppermute(shard, axis, pairs)  139 us
    reduce_scatter x1, waiting for transfers between devices, shards(): lax.psum_scatter(rows_product(hidden, grad_rows), 'dp', scatter_dimension...  92.5 us
    reduce_scatter x1, waiting for transfers between devices, shards(): lax.psum_scatter(rows_product(second_in, dpreact_b), 'dp', scatter_dimens...  91.6 us
    reduce_scatter x1, waiting for transfers between devices, shards(): lax.psum_scatter(rows_product(first_in, dfused_b), 'dp', scatter_dimensio...  77.3 us
    all_gather x1, waiting for transfers between devices, shards(): lax.all_gather(w_down, 'dp', axis=1, tiled=True)  66.6 us
    all_gather x1, waiting for transfers between devices, shards(): lax.all_gather(w_qkv, 'dp', axis=0, tiled=True)  44.5 us
    psum x1, blocking collectives, shards(): lax.psum((jnp.sum(dfirst * normed, axis=0), jnp.sum(dfirst, axis=0), jnp....  39.8 us
    reduce_scatter x1, waiting for transfers between devices, shards(): lax.psum_scatter(jnp.dot(context_b, full_out, preferred_element_type=jnp....  30.9 us
  transfers between devices with their start and end apart: 20, of which 14 were waited for; matrix products, arithmetic and copies ran while one was open for 12% of the time, Pallas kernels for 0%

commit v1 on v0

--- a/solution.py
+++ b/solution.py
@@ -105,7 +105,9 @@
     )
     row_count = first_in.shape[0]
     weights = (
-        lax.all_gather(w_qkv, "dp", axis=0, tiled=True),
+        jnp.concatenate(
+            lax.all_to_all(jnp.stack([w_qkv] * lax.axis_size("dp")), "dp", 0, 0), axis=0
+        ),
         lax.all_gather(w_out, "dp", axis=1, tiled=True),
         lax.all_gather(w_up, "dp", axis=0, tiled=True),
         lax.all_gather(w_down, "dp", axis=1, tiled=True),

time: 807 us -> 811 us (level)
  waiting for transfers between devices: 576 us -> 542 us
  blocking collectives: 87.3 us -> 115 us
    ppermute x8, waiting for transfers between devices: 139 us -> 216 us  [shifted_2(): return lax.ppermute(shard, axis, pairs)]
    all_gather x1, waiting for transfers between devices: 66.6 us -> 0.55 us  [shards(): lax.all_gather(w_down, 'dp', axis=1, tiled=True)]
    all_gather x1, waiting for transfers between devices: 44.5 us -> 0.02 us  [shards(): lax.all_gather(w_qkv, 'dp', axis=0, tiled=True)]
    all_gather x1, blocking collectives: 29.6 us -> 57.1 us  [shards(): lax.all_gather(w_out, 'dp', axis=1, tiled=True)]
  transfers between devices with their start and end apart: 20 -> 21, of which waited for: 14 -> 15; matrix products, arithmetic and copies ran while one was open for 12% -> 13% of each run, Pallas kernels for 0% -> 0%
where the time goes in v1:
time: 811 us; the launch traced here: 803 us
  waiting for transfers between devices  542 us (67%)
  blocking collectives  115 us (14%)
  matrix products  78 us (10%)
  other arithmetic  25.5 us (3%)
  starting transfers between devices  21.9 us (3%)
  between operations  15.2 us (2%)
    ppermute x8, waiting for transfers between devices, shifted_2(): return lax.ppermute(shard, axis, pairs)  216 us
    reduce_scatter x1, waiting for transfers between devices, shards(): lax.psum_scatter(rows_product(hidden, grad_rows), 'dp', scatter_dimension...  92.5 us
    reduce_scatter x1, waiting for transfers between devices, shards(): lax.psum_scatter(rows_product(second_in, dpreact_b), 'dp', scatter_dimens...  91.6 us
    reduce_scatter x1, waiting for transfers between devices, shards(): lax.psum_scatter(rows_product(first_in, dfused_b), 'dp', scatter_dimensio...  77.5 us
    all_gather x1, blocking collectives, shards(): lax.all_gather(w_out, 'dp', axis=1, tiled=True)  57.1 us
    psum x1, blocking collectives, shards(): lax.psum((jnp.sum(dfirst * normed, axis=0), jnp.sum(dfirst, axis=0), jnp....  39.8 us
    reduce_scatter x1, waiting for transfers between devices, shards(): lax.psum_scatter(jnp.dot(context_b, full_out, preferred_element_type=jnp....  30.9 us
    reduce_scatter x1, waiting for transfers between devices, shards(): lax.psum_scatter(rows_product(context_b, grad_rows), 'dp', scatter_dimens...  27.7 us
  transfers between devices with their start and end apart: 21, of which 15 were waited for; matrix products, arithmetic and copies ran while one was open for 13% of the time, Pallas kernels for 0%

profile of v1, /device:TPU:0, one launch (start us, length us, event | category | flops | bytes accessed | tf_op | source)
XLA Modules:
  0.0 802.5 jit_solution(16299015918187358122)
XLA Ops:
  10.2 2.0 fusion.55
  15.5 7.4 all-to-all-start
  23.9 57.1 %all_gather.25 = bf16[256,1024]{1,0:T(8,128)(2,1)S(1)} all-gather(bf16[256,128]{1,0:T(8,128)(2,1)S(1)} %copy-done.16), channel_id=1, replica_groups=mesh['dp'=8,'tensor'=4] {'dp'}, dimensions={1}, use_global_device_ids=true | all-gather | bytes 589824 | tf_op jit(solution)/shard_map/all_gather | solution.py:111
  81.0 1.9 fusion.39
  82.9 2.4 convolution_convert_fusion
  85.3 3.4 convolution_add_fusion.1
  88.7 1.9 copy.87
  92.3 3.0 collective-permute-start.1
  95.3 2.4 collective-permute-start.2
  97.7 1.9 collective-permute-start.3
  100.5 6.4 collective-permute-done
  107.9 10.6 %collective-permute-done.1 = bf16[2,512,256]{1,2,0:T(8,128)(2,1)S(1)} collective-permute-done((bf16[2,512,256]{1,2,0:T(8,128)(2,1)S(1)}, bf16[2,512,256]{1,2,0:T(8,128)(2,1)S(1)}, u32[]{:S(2)}, u32[]{:S(2)}) %collective-permute-start.1) | collective-permute-done | bytes 524320 | tf_op jit(solution)/shard_map/ppermute | solution.py:18
  119.4 15.8 %collective-permute-done.2 = bf16[2,512,256]{1,2,0:T(8,128)(2,1)S(1)} collective-permute-done((bf16[2,512,256]{1,2,0:T(8,128)(2,1)S(1)}, bf16[2,512,256]{1,2,0:T(8,128)(2,1)S(1)}, u32[]{:S(2)}, u32[]{:S(2)}) %collective-permute-start.2) | collective-permute-done | bytes 524320 | tf_op jit(solution)/shard_map/ppermute | solution.py:18
  136.2 4.6 collective-permute-done.3
  141.8 5.1 exponential_reduce_fusion.3
  152.0 2.0 multiply_reduce_fusion
  154.0 1.6 multiply_convert_fusion.4
  155.6 1.6 multiply_convert_fusion.3
  157.2 1.6 multiply_convert_fusion.1
  158.9 1.6 multiply_convert_fusion
  160.5 1.8 multiply_convert_fusion.2
  163.5 2.0 fusion.99
  184.3 8.8 %fusion.12 = (bf16[512,1024]{1,0:T(8,128)(2,1)}, f32[512,1024]{1,0:T(8,128)}) fusion(f32[1024]{0:T(1024)S(1)} %copy-done.25, bf16[512,1024]{1,0:T(8,128)(2,1)} %all-gather.9.cloned.1.call-done, bf16[1024,1024]{1,0:T(8,128)(2,1)} %all-gather.11.cloned.1.call-done), kind=kOutput, calls=%fused_computation.35 | convolution fusion | flops 1108344832 | bytes 6295552 | tf_op jit(solution)/shard_map/dot_general | solution.py:170
  193.7 4.2 fusion.129
  197.9 2.6 convolution_bitcast_fusion
  200.5 8.9 %collective-permute-done.4 = f32[2,512,256]{1,2,0:T(8,128)} collective-permute-done((f32[2,512,256]{1,2,0:T(8,128)S(1)}, f32[2,512,256]{1,2,0:T(8,128)}, u32[]{:S(2)}, u32[]{:S(2)}) %collective-permute-start.4) | collective-permute-done | bytes 1048608 | tf_op jit(solution)/shard_map/ppermute | solution.py:18
  209.4 47.0 %collective-permute-done.5 = f32[2,512,256]{1,2,0:T(8,128)} collective-permute-done((f32[2,512,256]{1,2,0:T(8,128)}, f32[2,512,256]{1,2,0:T(8,128)}, u32[]{:S(2)}, u32[]{:S(2)}) %collective-permute-start.5) | collective-permute-done | bytes 1048608 | tf_op jit(solution)/shard_map/ppermute | solution.py:18
  256.4 33.0 %collective-permute-done.6 = f32[2,512,256]{1,2,0:T(8,128)} collective-permute-done((f32[2,512,256]{1,2,0:T(8,128)}, f32[2,512,256]{1,2,0:T(8,128)}, u32[]{:S(2)}, u32[]{:S(2)}) %collective-permute-start.6) | collective-permute-done | bytes 1048608 | tf_op jit(solution)/shard_map/ppermute | solution.py:18
  289.4 89.9 %collective-permute-done.7 = f32[2,512,256]{1,2,0:T(8,128)} collective-permute-done((f32[2,512,256]{1,2,0:T(8,128)}, f32[2,512,256]{1,2,0:T(8,128)}, u32[]{:S(2)}, u32[]{:S(2)}) %collective-permute-start.7) | collective-permute-done | bytes 1048608 | tf_op jit(solution)/shard_map/ppermute | solution.py:18
  379.3 2.8 fusion.35
  383.3 2.6 convolution_bitcast_fusion.1
  385.9 2.3 pad_maximum_fusion
  388.3 3.2 fusion.133
  391.6 1.8 convolution_add_fusion
  393.4 2.4 fusion.137
  395.9 4.0 fusion.136
  400.0 4.9 fusion.69
  405.2 4.5 fusion.138
  410.0 17.9 %all-reduce.1 = (f32[768]{0:T(1024)}, f32[1024]{0:T(1024)}) all-reduce(f32[768]{0:T(1024)S(1)} %reduce_sum.170, f32[1024]{0:T(1024)S(1)} %get-tuple-element.85), channel_id=1, replica_groups=mesh['dp'=8,'tensor'=4] {'dp'}, use_global_device_ids=true, to_apply=%region_27.28 | all-reduce | flops 1792 | bytes 14336 | tf_op jit(solution)/shard_map/psum | solution.py:260
  428.0 2.0 reduce-scatter.9.cloned.1.call-done
  431.3 1.5 fusion.120
  432.8 30.9 %reduce-scatter.7.cloned.1.call-done = f32[128,1024]{1,0:T(8,128)} async-done(((f32[512,1024]{1,0:T(8,128)}), f32[128,1024]{1,0:T(8,128)}) %reduce-scatter.7.cloned.1.call-update) | async-done | bytes 524304 | tf_op jit(solution)/shard_map/reduce_scatter | solution.py:172
  463.7 2.1 convert_reduce_fusion.1
  465.8 39.8 %all-reduce = (f32[1024]{0:T(1024)}, f32[1024]{0:T(1024)}, f32[1024]{0:T(1024)}, f32[1024]{0:T(1024)}, f32[1024]{0:T(1024)S(1)}) all-reduce(f32[1024]{0:T(1024)S(1)} %get-tuple-element.20, f32[1024]{0:T(1024)S(1)} %get-tuple-element.17, f32[1024]{0:T(1024)S(1)} %get-tuple-element.21, ...), channel_id=1, replica_groups=mesh['dp'=8,'tensor'=4] {'dp','tensor'}, use_global_device_ids=true, to_apply=%region_18.19 | all-reduce | flops 5120 | bytes 40960 | tf_op jit(solution)/shard_map/psum | solution.py:261
  505.6 27.7 %reduce-scatter.13.cloned.1.call-done = f32[256,128]{1,0:T(8,128)} async-done(((f32[256,1024]{1,0:T(8,128)}), f32[256,128]{1,0:T(8,128)}) %reduce-scatter.13.cloned.1.call-update) | async-done | bytes 131088 | tf_op jit(solution)/shard_map/reduce_scatter | solution.py:196
  533.3 77.5 %reduce-scatter.11.cloned.1.call-done = f32[128,768]{1,0:T(8,128)} async-done(((f32[1024,768]{1,0:T(8,128)}), f32[128,768]{1,0:T(8,128)}) %reduce-scatter.11.cloned.1.call-update) | async-done | bytes 393232 | tf_op jit(solution)/shard_map/reduce_scatter | solution.py:257
  610.8 91.6 %reduce-scatter.15.cloned.1.call-done = f32[128,1024]{1,0:T(8,128)} async-done(((f32[1024,1024]{1,0:T(8,128)}), f32[128,1024]{1,0:T(8,128)}) %reduce-scatter.15.cloned.1.call-update) | async-done | bytes 524304 | tf_op jit(solution)/shard_map/reduce_scatter | solution.py:197
  702.4 92.5 %reduce-scatter.17.cloned.1.call-done = f32[1024,128]{1,0:T(8,128)} async-done(((f32[1024,1024]{1,0:T(8,128)}), f32[1024,128]{1,0:T(8,128)}) %reduce-scatter.17.cloned.1.call-update) | async-done | bytes 524304 | tf_op jit(solution)/shard_map/reduce_scatter | solution.py:198
  (164 shorter events, 42.6 us)
Async XLA Ops:
  7.2 7.0 copy-start.10
  7.2 75.7 %all-gather.15.cloned.1.call-start = ((), (), s32[]{:S(2)}) async-start(), calls=%async_computation.12 | async-start | bytes 1310720 | tf_op jit(solution)/shard_map/all_gather | solution.py:180
  7.9 77.4 %all-gather.7.cloned.1.call-start = ((), (), s32[]{:S(2)}) async-start(), calls=%async_computation.7 | async-start | bytes 1310720 | tf_op jit(solution)/shard_map/all_gather | solution.py:99
  12.3 172.0 %all-gather.9.cloned.1.call-start = ((), (), s32[]{:S(2)}) async-start(), calls=%async_computation.8 | async-start | bytes 1310720 | tf_op jit(solution)/shard_map/all_gather | solution.py:102
  13.0 171.3 %all-gather.11.cloned.1.call-start = ((), (), s32[]{:S(2)}) async-start(), calls=%async_computation.9 | async-start | bytes 2359296 | tf_op jit(solution)/shard_map/all_gather | solution.py:112
  13.6 180.1 %all-gather.13.cloned.1.call-start = ((), (), s32[]{:S(2)}) async-start(), calls=%async_computation.10 | async-start | bytes 2359296 | tf_op jit(solution)/shard_map/all_gather | solution.py:113
  15.5 8.1 %copy-start.19 = (s32[512]{0:T(512)S(1)}, s32[512]{0:T(512)}, u32[]{:S(2)}) copy-start(s32[512]{0:T(512)} %param.16) | copy-start | bytes 6148
  15.5 8.4 %copy-start.16 = (bf16[256,128]{1,0:T(8,128)(2,1)S(1)}, bf16[256,128]{1,0:T(8,128)(2,1)}, u32[]{:S(2)}) copy-start(bf16[256,128]{1,0:T(8,128)(2,1)} %param.23) | copy-start | bytes 196612
  15.5 69.9 %all-to-all-start = ((bf16[8,128,768]{2,1,0:T(8,128)(2,1)}), bf16[8,128,768]{2,1,0:T(8,128)(2,1)S(1)}, u32[]{:S(2)}, u32[]{:S(2)}) async-start(bf16[8,128,768]{2,1,0:T(8,128)(2,1)} %stack.47), calls=%async_computation | async-start | bytes 3145728 | tf_op jit(solution)/shard_map/all_to_all | solution.py:109
  22.9 62.4 %copy-start.24 = (f32[768]{0:T(1024)S(1)}, f32[768]{0:T(1024)}, u32[]{:S(2)}) copy-start(f32[768]{0:T(1024)} %param.22) | copy-start | bytes 9220
  22.9 360.4 %all-gather.17.cloned.1.call-start = ((), (), s32[]{:S(2)}) async-start(), calls=%async_computation.13 | async-start | bytes 1769472 | tf_op jit(solution)/shard_map/all_gather | solution.py:182
  23.5 406.5 %reduce-scatter.9.cloned.1.call-start = ((), (), s32[]{:S(2)}) async-start(), calls=%async_computation.14 | async-start | bytes 5242880 | tf_op jit(solution)/shard_map/reduce_scatter | solution.py:241
  23.8 75.7 %copy-start.12 = (f32[512,16]{0,1:T(8,128)}, f32[512,16]{0,1:T(8,128)S(1)}, u32[]{:S(2)}) copy-start(f32[512,16]{0,1:T(8,128)S(1)} %get-tuple-element.99) | copy-start | bytes 98308
  23.8 75.7 %copy-start.14 = (f32[512,16]{0,1:T(8,128)}, f32[512,16]{0,1:T(8,128)S(1)}, u32[]{:S(2)}) copy-start(f32[512,16]{0,1:T(8,128)S(1)} %get-tuple-element.100) | copy-start | bytes 98308
  80.9 4.4 copy-start.2
  91.0 15.9 %collective-permute-start = (bf16[2,512,256]{1,2,0:T(8,128)(2,1)S(1)}, bf16[2,512,256]{1,2,0:T(8,128)(2,1)S(1)}, u32[]{:S(2)}, u32[]{:S(2)}) collective-permute-start(bf16[2,512,256]{1,2,0:T(8,128)(2,1)S(1)} %pad_maximum_fusion.6), channel_id=1, source_target_pairs={{0,4},{4,8},{8,12},{12,16},{16,20},{20,24},{24,28},{1,5},{5,9},{9,... | collective-permute-start | bytes 1572872 | tf_op jit(solution)/shard_map/ppermute | solution.py:18
  92.3 26.2 %collective-permute-start.1 = (bf16[2,512,256]{1,2,0:T(8,128)(2,1)S(1)}, bf16[2,512,256]{1,2,0:T(8,128)(2,1)S(1)}, u32[]{:S(2)}, u32[]{:S(2)}) collective-permute-start(bf16[2,512,256]{1,2,0:T(8,128)(2,1)S(1)} %pad_maximum_fusion.6), channel_id=1, source_target_pairs={{0,8},{4,12},{8,16},{12,20},{16,24},{20,28},{1,9},{5,13},{9,17},{1... | collective-permute-start | bytes 1572872 | tf_op jit(solution)/shard_map/ppermute | solution.py:18
  95.3 39.9 %collective-permute-start.2 = (bf16[2,512,256]{1,2,0:T(8,128)(2,1)S(1)}, bf16[2,512,256]{1,2,0:T(8,128)(2,1)S(1)}, u32[]{:S(2)}, u32[]{:S(2)}) collective-permute-start(bf16[2,512,256]{1,2,0:T(8,128)(2,1)S(1)} %pad_maximum_fusion.6), channel_id=1, source_target_pairs={{0,12},{4,16},{8,20},{12,24},{16,28},{1,13},{5,17},{9,21},{13,25},... | collective-permute-start | bytes 1572872 | tf_op jit(solution)/shard_map/ppermute | solution.py:18
  97.7 43.2 %collective-permute-start.3 = (bf16[2,512,256]{1,2,0:T(8,128)(2,1)S(1)}, bf16[2,512,256]{1,2,0:T(8,128)(2,1)S(1)}, u32[]{:S(2)}, u32[]{:S(2)}) collective-permute-start(bf16[2,512,256]{1,2,0:T(8,128)(2,1)S(1)} %pad_maximum_fusion.6), channel_id=1, source_target_pairs={{0,16},{4,20},{8,24},{12,28},{1,17},{5,21},{9,25},{13,29},{2,18},{... | collective-permute-start | bytes 1572872 | tf_op jit(solution)/shard_map/ppermute | solution.py:18
  118.5 0.9 copy-start.6
  150.7 1.3 copy-start.26
  174.4 35.0 %collective-permute-start.4 = (f32[2,512,256]{1,2,0:T(8,128)S(1)}, f32[2,512,256]{1,2,0:T(8,128)}, u32[]{:S(2)}, u32[]{:S(2)}) collective-permute-start(f32[2,512,256]{1,2,0:T(8,128)S(1)} %pad_maximum_fusion.2), channel_id=1, source_target_pairs={{4,0},{8,4},{12,8},{16,12},{20,16},{24,20},{28,24},{5,1},{9,5},{13... | collective-permute-start | bytes 3145736 | tf_op jit(solution)/shard_map/ppermute | solution.py:18
  177.5 78.9 %collective-permute-start.5 = (f32[2,512,256]{1,2,0:T(8,128)}, f32[2,512,256]{1,2,0:T(8,128)}, u32[]{:S(2)}, u32[]{:S(2)}) collective-permute-start(f32[2,512,256]{1,2,0:T(8,128)} %pad_maximum_fusion.3), channel_id=1, source_target_pairs={{8,0},{12,4},{16,8},{20,12},{24,16},{28,20},{9,1},{13,5},{17,9},{2... | collective-permute-start | bytes 3145736 | tf_op jit(solution)/shard_map/ppermute | solution.py:18
  178.8 4.9 copy-start.7
  179.9 109.5 %collective-permute-start.6 = (f32[2,512,256]{1,2,0:T(8,128)}, f32[2,512,256]{1,2,0:T(8,128)}, u32[]{:S(2)}, u32[]{:S(2)}) collective-permute-start(f32[2,512,256]{1,2,0:T(8,128)} %pad_maximum_fusion.4), channel_id=1, source_target_pairs={{12,0},{16,4},{20,8},{24,12},{28,16},{13,1},{17,5},{21,9},{25,13},... | collective-permute-start | bytes 3145736 | tf_op jit(solution)/shard_map/ppermute | solution.py:18
  182.3 2.0 copy-start.25
  182.3 197.0 %collective-permute-start.7 = (f32[2,512,256]{1,2,0:T(8,128)}, f32[2,512,256]{1,2,0:T(8,128)}, u32[]{:S(2)}, u32[]{:S(2)}) collective-permute-start(f32[2,512,256]{1,2,0:T(8,128)} %pad_maximum_fusion.5), channel_id=1, source_target_pairs={{16,0},{20,4},{24,8},{28,12},{17,1},{21,5},{25,9},{29,13},{18,2},{... | collective-permute-start | bytes 3145736 | tf_op jit(solution)/shard_map/ppermute | solution.py:18
  184.2 9.5 %copy-start.1 = (bf16[512,1024]{1,0:T(8,128)(2,1)S(1)}, bf16[512,1024]{1,0:T(8,128)(2,1)}, u32[]{:S(2)}) copy-start(bf16[512,1024]{1,0:T(8,128)(2,1)} %all-gather.15.cloned.1.call-done) | copy-start | bytes 3145732
  193.7 4.2 copy-start.23
  197.9 2.7 copy-start.9
  197.9 181.4 %copy-start.11 = (f32[4,64,512]{2,1,0:T(8,128)S(1)}, f32[4,64,512]{2,1,0:T(8,128)}, u32[]{:S(2)}) copy-start(f32[4,64,512]{2,1,0:T(8,128)} %fusion.99) | copy-start | bytes 1572868
  382.1 0.8 copy-start.15
  382.1 0.8 copy-start.13
  383.3 2.6 copy-start.4
  388.2 75.5 %reduce-scatter.7.cloned.1.call-start = ((), (), s32[]{:S(2)}) async-start(), calls=%async_computation.11 | async-start | bytes 2621440 | tf_op jit(solution)/shard_map/reduce_scatter | solution.py:172
  388.3 3.3 copy-start.3
  388.3 3.3 copy-start.5
  393.4 140.0 %reduce-scatter.13.cloned.1.call-start = ((), (), s32[]{:S(2)}) async-start(), calls=%async_computation.16 | async-start | bytes 1179648 | tf_op jit(solution)/shard_map/reduce_scatter | solution.py:196
  395.9 214.9 %reduce-scatter.11.cloned.1.call-start = ((), (), s32[]{:S(2)}) async-start(), calls=%async_computation.15 | async-start | bytes 3538944 | tf_op jit(solution)/shard_map/reduce_scatter | solution.py:257
  399.9 302.5 %reduce-scatter.15.cloned.1.call-start = ((), (), s32[]{:S(2)}) async-start(), calls=%async_computation.17 | async-start | bytes 4718592 | tf_op jit(solution)/shard_map/reduce_scatter | solution.py:197
  405.0 389.9 %reduce-scatter.17.cloned.1.call-start = ((), (), s32[]{:S(2)}) async-start(), calls=%async_computation.18 | async-start | bytes 4718592 | tf_op jit(solution)/shard_map/reduce_scatter | solution.py:198
  409.7 21.6 %copy-start = (bf16[128,1024]{1,0:T(8,128)(2,1)S(1)}, bf16[128,1024]{1,0:T(8,128)(2,1)}, u32[]{:S(2)}) copy-start(bf16[128,1024]{1,0:T(8,128)(2,1)} %param.15) | copy-start | bytes 786436
  409.7 21.6 %copy-start.17 = (f32[1024]{0:T(1024)S(1)}, f32[1024]{0:T(1024)}, u32[]{:S(2)}) copy-start(f32[1024]{0:T(1024)} %param.17) | copy-start | bytes 12292
  409.7 21.6 %copy-start.18 = (f32[1024]{0:T(1024)S(1)}, f32[1024]{0:T(1024)}, u32[]{:S(2)}) copy-start(f32[1024]{0:T(1024)} %param.19) | copy-start | bytes 12292
  409.7 54.0 %copy-start.8 = (bf16[128,1024]{1,0:T(8,128)(2,1)S(1)}, bf16[128,1024]{1,0:T(8,128)(2,1)}, u32[]{:S(2)}) copy-start(bf16[128,1024]{1,0:T(8,128)(2,1)} %param.29) | copy-start | bytes 786436
  409.7 54.0 %copy-start.20 = (f32[1024]{0:T(1024)S(1)}, f32[1024]{0:T(1024)}, u32[]{:S(2)}) copy-start(f32[1024]{0:T(1024)} %param.28) | copy-start | bytes 12292
  409.7 54.0 %copy-start.21 = (f32[1024]{0:T(1024)S(1)}, f32[1024]{0:T(1024)}, u32[]{:S(2)}) copy-start(f32[1024]{0:T(1024)} %param.24) | copy-start | bytes 12292
  505.6 289.9 %copy-start.22 = (f32[1024]{0:T(1024)}, f32[1024]{0:T(1024)S(1)}, u32[]{:S(2)}) copy-start(f32[1024]{0:T(1024)S(1)} %get-tuple-element.130) | copy-start | bytes 12292
Sparse Core Ops, SparseCore 0:
  9.6 19.4 all-gather.14
  31.1 16.6 all-gather.6
  50.0 16.6 all-gather.8
  68.7 60.8 all-gather.10
  131.5 62.1 all-gather.12
  195.7 57.0 all-gather.16
  388.4 41.5 reduce-scatter.8
  432.5 31.1 reduce-scatter.6
  467.7 65.6 reduce-scatter.12
  537.3 73.4 reduce-scatter.10
  615.0 87.3 reduce-scatter.14
  706.5 88.3 reduce-scatter.16
